TPU v7x, 128 devices: a whole 4x4x4 slice. The times are simulated.
128 devices in a mesh: gx: 8 (over x, core), gy: 4 (over z), band: 4 (over y).
Axes of the slice: x: 4, y: 4, z: 4, core: 2. Of those that a mesh axis runs over, the one named last changes fastest.
Arguments:
- block: float32 [32, 96, 18432], P('band', 'gx', 'gy'), may hold values from -9 to 9
- prior: float32 [256, 96, 18432], P('band', 'gx', 'gy'), may hold values from -9 to 9
- potential: float32 [96, 18432], P('gx', 'gy'), may hold values from -1.5 to 1
Outputs:
- orbitals: float32 [32, 96, 18432], P('band', 'gx', 'gy')
All inputs are finite; a program needn't handle non-finite values.
Results may differ from a plain program's by a relative error of at most 0.000098.
Values sent between devices are 32-bit elements; how exact they have to be, the bound alone decides.
A program may use at most 128 MiB of HBM per device.

v0:
```python
import jax
import jax.numpy as jnp
from jax import lax
from jax.sharding import PartitionSpec as P

NZ = 192
coeffs = (-205.0 / 72.0, 8.0 / 5.0, -1.0 / 5.0, 8.0 / 315.0, -1.0 / 560.0)


def extended_2(x, sides, width):
    for axis, dim in sides:
        devices, length = (lax.axis_size(axis), x.shape[dim])
        up = [(i, (i + 1) % devices) for i in range(devices - 1)]
        down = [(j, i) for i, j in up]
        last = lax.slice_in_dim(x, length - width, length, axis=dim)
        leading = lax.slice_in_dim(x, 0, width, axis=dim)
        before = lax.ppermute(last, axis, up)
        after = lax.ppermute(leading, axis, down)
        x = jnp.concatenate([before, x, after], axis=dim)
    return x


def laplace(padded):
    center = padded[:, 4:-4, 4:-4, 4:-4]
    total = 3.0 * coeffs[0] * center
    for shift in range(1, 5):
        total = total + coeffs[shift] * (
            padded[:, 4 + shift : padded.shape[1] - 4 + shift, 4:-4, 4:-4]
            + padded[:, 4 - shift : padded.shape[1] - 4 - shift, 4:-4, 4:-4]
        )
        total = total + coeffs[shift] * (
            padded[:, 4:-4, 4 + shift : padded.shape[2] - 4 + shift, 4:-4]
            + padded[:, 4:-4, 4 - shift : padded.shape[2] - 4 - shift, 4:-4]
        )
        total = total + coeffs[shift] * (
            padded[:, 4:-4, 4:-4, 4 + shift : padded.shape[3] - 4 + shift]
            + padded[:, 4:-4, 4:-4, 4 - shift : padded.shape[3] - 4 - shift]
        )
    return total


def matmul(left, right):
    return jnp.dot(left, right, precision=lax.Precision.HIGHEST, preferred_element_type=jnp.float32)


def shards(block, prior, potential):
    own_count = block.shape[0]
    rows_x = block.shape[1]
    rows_y = block.shape[2] // NZ
    total_count = own_count * lax.axis_size("band")
    ncells_all = rows_x * lax.axis_size("gx") * rows_y * lax.axis_size("gy") * NZ
    grid_block = block.reshape(own_count, rows_x, rows_y, NZ)
    extended = extended_2(grid_block, (("gx", 1), ("gy", 2)), 4)
    extended = jnp.pad(extended, ((0, 0), (0, 0), (0, 0), (4, 4)))
    lap_flat = laplace(extended).reshape(block.shape)
    phi = -2.0 * lap_flat + potential[None] * block
    phi_flat = phi.reshape(own_count, -1)
    prior_flat = prior.reshape(prior.shape[0], -1)
    phi_all = lax.all_gather(phi_flat, "band", axis=0, tiled=True)
    correlation = lax.psum(matmul(prior_flat, phi_all.T), ("gx", "gy")) / ncells_all
    removed = lax.psum_scatter(
        matmul(correlation.T, prior_flat), "band", scatter_dimension=0, tiled=True
    )
    projected_own = phi_flat - removed
    projected = lax.all_gather(projected_own, "band", axis=0, tiled=True)
    gram = lax.psum(matmul(projected, projected.T), ("gx", "gy")) / ncells_all
    lower = jnp.linalg.cholesky(gram)
    inverse = lax.linalg.triangular_solve(
        lower, jnp.eye(total_count, dtype=lower.dtype), left_side=True, lower=True
    )
    first_row = lax.axis_index("band") * own_count
    own_rows = lax.dynamic_slice_in_dim(inverse, first_row, own_count, 0)
    orbitals = matmul(own_rows, projected)
    return orbitals.reshape(block.shape)


def solution(mesh):
    in_specs = (P("band", "gx", "gy"), P("band", "gx", "gy"), P("gx", "gy"))
    out_specs = P("band", "gx", "gy")
    return jax.shard_map(shards, mesh=mesh, in_specs=in_specs, out_specs=out_specs, check_vma=False)
```

profile of v0, /device:TPU:0, one launch (start us, length us, event | category | flops | bytes accessed | tf_op | source)
XLA Modules:
  0.0 602.9 jit_solution(7956143481172874915)
XLA Ops:
  6.5 2.0 reshape.25
  8.7 1.3 collective-permute-start.1
  10.0 1.3 collective-permute-start
  12.9 3.1 collective-permute-done
  17.7 4.6 collective-permute-start.3
  22.3 6.6 %collective-permute-done.2 = f32[8,20,4,192]{3,2,0,1:T(4,128)S(1)} collective-permute-done((f32[8,20,4,192]{3,2,0,1:T(4,128)S(1)}, f32[8,20,4,192]{3,2,0,1:T(4,128)S(1)}, u32[]{:S(2)}, u32[]{:S(2)}) %collective-permute-start.2) | collective-permute-done | bytes 491552 | tf_op jit(solution)/shard_map/ppermute | solution.py:18
  28.9 1.5 collective-permute-done.3
  30.3 2.9 select_maximum_fusion
  33.2 20.7 %fusion.9 = f32[8,12,24,192]{3,2,0,1:T(8,128)} fusion(f32[8,20,24,192]{3,2,0,1:T(8,128)} %copy-done.3, f32[8,20,4,192]{3,2,0,1:T(4,128)S(1)} %collective-permute-done.3, f32[8,20,4,192]{3,2,0,1:T(4,128)S(1)} %collective-permute-done.2, f32[8,20,32,200]{3,2,0,1:T(8,128)S(1)} %select_maximum_fusion, f32[8,16,24,192]{3,2,0,1:T(8,128)} %copy-done.1, ...), kind=kLoop, calls=%fused_computation.25 | loop fusion | flops 20348928 | bytes 35782656 | tf_op jit(solution)/shard_map/mul | solution.py:56
  53.9 2.3 mul.78
  56.2 2.4 multiply_add_fusion
  58.9 11.4 %copy.10 = f32[12,8,8,4608]{3,2,0,1:T(8,128)} copy(f32[12,8,8,4608]{3,2,1,0:T(8,128)} %bitcast.31) | data formatting | bytes 28311552 | tf_op jit(solution)/shard_map/reshape | solution.py:58
  70.3 79.2 %all-gather.3.cloned.1.call-done = f32[32,55296]{1,0:T(8,128)} async-done(((f32[8,55296]{1,0:T(8,128)}), f32[32,55296]{1,0:T(8,128)}) %all-gather.3.cloned.1.call-update) | async-done | bytes 7077904 | tf_op jit(solution)/shard_map/all_gather | solution.py:59
  149.5 14.5 %convolution_bitcast_fusion = f32[64,32]{0,1:T(8,128)S(1)} fusion(f32[32,55296]{1,0:T(8,128)} %all-gather.3.cloned.1.call-done, f32[64,55296]{1,0:T(8,128)} %bitcast.27), kind=kOutput, calls=%fused_computation.63 | convolution fusion | flops 1358954496 | bytes 21241856 | tf_op jit(solution)/shard_map/dot_general | solution.py:43
  164.0 128.3 %psum.14 = f32[64,32]{0,1:T(8,128)S(1)} all-reduce(f32[64,32]{0,1:T(8,128)S(1)} %convolution_bitcast_fusion), channel_id=1, replica_groups=mesh['gx'=8,'gy'=4,'band'=4] {'gx','gy'}, use_global_device_ids=true, to_apply=%region_0.1 | all-reduce | flops 2048 | bytes 16384 | tf_op jit(solution)/shard_map/psum | solution.py:60
  292.3 11.7 %fusion.40 = f32[32,55296]{1,0:T(8,128)} fusion(f32[64,55296]{1,0:T(8,128)} %bitcast.28, f32[64,32]{0,1:T(8,128)S(1)} %psum.14), kind=kOutput, calls=%fused_computation.78 | convolution fusion | flops 1358956544 | bytes 21241856 | tf_op jit(solution)/shard_map/dot_general | solution.py:43
  304.0 66.2 %reduce-scatter.2.cloned.1.call-done = f32[8,55296]{1,0:T(8,128)} async-done(((f32[32,55296]{1,0:T(8,128)}), f32[8,55296]{1,0:T(8,128)}) %reduce-scatter.2.cloned.1.call-update) | async-done | bytes 1769488 | tf_op jit(solution)/shard_map/reduce_scatter | solution.py:61
  370.3 2.9 sub.3
  373.1 72.1 %all-gather.5.cloned.1.call-done = f32[32,55296]{1,0:T(8,128)} async-done(((f32[8,55296]{1,0:T(8,128)}), f32[32,55296]{1,0:T(8,128)}) %all-gather.5.cloned.1.call-update) | async-done | bytes 7077904 | tf_op jit(solution)/shard_map/all_gather | solution.py:65
  445.3 9.1 %fusion.49 = f32[32,32]{0,1:T(8,128)S(1)} fusion(f32[32,55296]{1,0:T(8,128)} %all-gather.5.cloned.1.call-done), kind=kOutput, calls=%fused_computation.91 | convolution fusion | flops 679477248 | bytes 7081984 | tf_op jit(solution)/shard_map/dot_general | solution.py:43
  454.4 128.5 %psum.15 = f32[32,32]{0,1:T(8,128)S(1)} all-reduce(f32[32,32]{0,1:T(8,128)S(1)} %fusion.49), channel_id=1, replica_groups=mesh['gx'=8,'gy'=4,'band'=4] {'gx','gy'}, use_global_device_ids=true, to_apply=%region_2.3 | all-reduce | flops 1024 | bytes 8192 | tf_op jit(solution)/shard_map/psum | solution.py:66
  583.0 2.9 cholesky.17
  587.2 2.4 custom-call.6
  589.9 6.5 %fusion.43 = f32[8,55296]{1,0:T(8,128)} fusion(f32[32,55296]{1,0:T(8,128)} %all-gather.5.cloned.1.call-done, f32[32,32]{1,0:T(8,128)S(1)} %fusion.37, s32[]{:T(128)S(6)} %select_n.8), kind=kOutput, calls=%fused_computation.84 | convolution fusion | flops 169869312 | bytes 8851460 | tf_op jit(solution)/shard_map/dot_general | solution.py:43
  (32 shorter events, 5.3 us)
Async XLA Ops:
  6.5 142.9 %all-gather.3.cloned.1.call-start = ((), (), s32[]{:S(2)}) async-start(), calls=%async_computation.1 | async-start | bytes 8847360 | tf_op jit(solution)/shard_map/all_gather | solution.py:59
  8.5 3.5 copy-start.2
  8.7 3.2 collective-permute-start.1
  10.0 5.9 collective-permute-start
  12.9 3.5 copy-start.1
  16.1 17.1 %copy-start = (f32[8,16,24,192]{3,2,0,1:T(8,128)}, f32[8,16,24,192]{3,2,0,1:T(8,128)S(1)}, u32[]{:S(2)}) copy-start(f32[8,16,24,192]{3,2,0,1:T(8,128)S(1)} %get-tuple-element.12) | copy-start | bytes 7077892
  16.1 17.1 %copy-start.3 = (f32[8,20,24,192]{3,2,0,1:T(8,128)}, f32[8,20,24,192]{3,2,0,1:T(8,128)S(1)}, u32[]{:S(2)}) copy-start(f32[8,20,24,192]{3,2,0,1:T(8,128)S(1)} %get-tuple-element.13) | copy-start | bytes 8847364
  16.4 12.5 %collective-permute-start.2 = (f32[8,20,4,192]{3,2,0,1:T(4,128)S(1)}, f32[8,20,4,192]{3,2,0,1:T(4,128)S(1)}, u32[]{:S(2)}, u32[]{:S(2)}) collective-permute-start(f32[8,20,4,192]{3,2,0,1:T(4,128)S(1)} %get-tuple-element.5), channel_id=1, source_target_pairs={{4,0},{8,4},{12,8},{5,1},{9,5},{13,9},{6,2},{10,6},{14,10},{7,3},{... | collective-permute-start | bytes 1474568 | tf_op jit(solution)/shard_map/ppermute | solution.py:18
  17.7 12.6 %collective-permute-start.3 = (f32[8,20,4,192]{3,2,0,1:T(4,128)S(1)}, f32[8,20,4,192]{3,2,0,1:T(4,128)S(1)}, u32[]{:S(2)}, u32[]{:S(2)}) collective-permute-start(f32[8,20,4,192]{3,2,0,1:T(4,128)S(1)} %get-tuple-element.6), channel_id=1, source_target_pairs={{0,4},{4,8},{8,12},{1,5},{5,9},{9,13},{2,6},{6,10},{10,14},{3,7},{... | collective-permute-start | bytes 1474568 | tf_op jit(solution)/shard_map/ppermute | solution.py:17
  53.9 2.3 copy-start.5
  58.7 311.6 %reduce-scatter.2.cloned.1.call-start = ((), (), s32[]{:S(2)}) async-start(), calls=%async_computation.2 | async-start | bytes 8847360 | tf_op jit(solution)/shard_map/reduce_scatter | solution.py:61
  304.0 66.3 %copy-start.4 = (f32[8,12,4608]{2,0,1:T(8,128)S(1)}, f32[8,12,4608]{2,0,1:T(8,128)}, u32[]{:S(2)}) copy-start(f32[8,12,4608]{2,0,1:T(8,128)} %multiply_add_fusion) | copy-start | bytes 5308420
  304.0 141.3 %all-gather.5.cloned.1.call-start = ((), (), s32[]{:S(2)}) async-start(), calls=%async_computation.3 | async-start | bytes 8847360 | tf_op jit(solution)/shard_map/all_gather | solution.py:65
Sparse Core Ops, SparseCore 0:
  58.8 90.6 all-gather.2
  304.1 66.1 reduce-scatter.1
  373.3 71.9 all-gather.4
where the time goes:
time: 603 us
  blocking collectives  257 us (43%)
  waiting for transfers between devices  229 us (38%)
  matrix products  42 us (7%)
  other arithmetic  35.5 us (6%)
  local copies, waits for them, and re-layouts  17.2 us (3%)
  between operations  13.3 us (2%)
  starting transfers between devices  8.78 us (1%)
    psum x1, blocking collectives, shards(): gram = lax.psum(matmul(projected, projected.T), ('gx', 'gy')) / ncells_all  129 us
    psum x1, blocking collectives, shards(): lax.psum(matmul(prior_flat, phi_all.T), ('gx', 'gy')) / ncells_all  128 us
    all_gather x1, waiting for transfers between devices, shards(): phi_all = lax.all_gather(phi_flat, 'band', axis=0, tiled=True)  79.2 us
    all_gather x1, waiting for transfers between devices, shards(): projected = lax.all_gather(projected_own, 'band', axis=0, tiled=True)  72.1 us
    reduce_scatter x1, waiting for transfers between devices, shards(): lax.psum_scatter(matmul(correlation.T, prior_flat), 'band', scatter_dimen...  66.2 us
    dot_general x4, matrix products, matmul(): jnp.dot(left, right, precision=lax.Precision.HIGHEST, preferred_element_t...  41.8 us
    mul x1, other arithmetic, shards(): phi = -2.0 * lap_flat + potential[None] * block  20.7 us
  transfers between devices with their start and end apart: 7, of which 7 were waited for; matrix products, arithmetic and copies ran while one was open for 2% of the time, Pallas kernels for 0%

commit v1 on v0

--- a/solution.py
+++ b/solution.py
@@ -63,7 +63,7 @@
     )
     projected_own = phi_flat - removed
     projected = lax.all_gather(projected_own, "band", axis=0, tiled=True)
-    gram = lax.psum(matmul(projected, projected.T), ("gx", "gy")) / ncells_all
+    gram = lax.psum(lax.psum(matmul(projected, projected.T), "gx"), "gy") / ncells_all
     lower = jnp.linalg.cholesky(gram)
     inverse = lax.linalg.triangular_solve(
         lower, jnp.eye(total_count, dtype=lower.dtype), left_side=True, lower=True

time: 603 us -> 517 us (0.86)
  blocking collectives: 257 us -> 171 us
    psum x1 -> x2, blocking collectives: 129 us -> 42.6 us  [the longest x1 25.5 us: shards(): lax.psum(matmul(projected, projected.T), 'gx')]
where the time goes in v1:
time: 517 us
  waiting for transfers between devices  229 us (44%)
  blocking collectives  171 us (33%)
  matrix products  42 us (8%)
  other arithmetic  35.5 us (7%)
  local copies, waits for them, and re-layouts  17.2 us (3%)
  between operations  13.3 us (3%)
  starting transfers between devices  8.78 us (2%)
    psum x1, blocking collectives, shards(): lax.psum(matmul(prior_flat, phi_all.T), ('gx', 'gy')) / ncells_all  128 us
    all_gather x1, waiting for transfers between devices, shards(): phi_all = lax.all_gather(phi_flat, 'band', axis=0, tiled=True)  79.2 us
    all_gather x1, waiting for transfers between devices, shards(): projected = lax.all_gather(projected_own, 'band', axis=0, tiled=True)  72.1 us
    reduce_scatter x1, waiting for transfers between devices, shards(): lax.psum_scatter(matmul(correlation.T, prior_flat), 'band', scatter_dimen...  66.2 us
    dot_general x4, matrix products, matmul(): jnp.dot(left, right, precision=lax.Precision.HIGHEST, preferred_element_t...  41.8 us
    psum x1, blocking collectives, shards(): lax.psum(matmul(projected, projected.T), 'gx')  25.5 us
    mul x1, other arithmetic, shards(): phi = -2.0 * lap_flat + potential[None] * block  20.6 us
    psum x1, blocking collectives, shards(): lax.psum(lax.psum(matmul(projected, projected.T), 'gx'), 'gy') / ncells_all  17.1 us
  transfers between devices with their start and end apart: 7, of which 7 were waited for; matrix products, arithmetic and copies ran while one was open for 2% of the time, Pallas kernels for 0%

profile of v1, /device:TPU:0, one launch (start us, length us, event | category | flops | bytes accessed | tf_op | source)
XLA Modules:
  0.0 517.0 jit_solution(8330332708660640242)
XLA Ops:
  6.5 2.0 reshape.25
  8.7 1.3 collective-permute-start.1
  12.9 3.1 collective-permute-done
  17.7 4.6 collective-permute-start.3
  22.3 6.6 %collective-permute-done.2 = f32[8,20,4,192]{3,2,0,1:T(4,128)S(1)} collective-permute-done((f32[8,20,4,192]{3,2,0,1:T(4,128)S(1)}, f32[8,20,4,192]{3,2,0,1:T(4,128)S(1)}, u32[]{:S(2)}, u32[]{:S(2)}) %collective-permute-start.2) | collective-permute-done | bytes 491552 | tf_op jit(solution)/shard_map/ppermute | solution.py:18
  28.9 1.5 collective-permute-done.3
  30.3 2.9 select_maximum_fusion
  33.2 20.6 %fusion.9 = f32[8,12,24,192]{3,2,0,1:T(8,128)} fusion(f32[8,20,24,192]{3,2,0,1:T(8,128)} %copy-done.3, f32[8,20,4,192]{3,2,0,1:T(4,128)S(1)} %collective-permute-done.3, f32[8,20,4,192]{3,2,0,1:T(4,128)S(1)} %collective-permute-done.2, f32[8,20,32,200]{3,2,0,1:T(8,128)S(1)} %select_maximum_fusion, f32[8,16,24,192]{3,2,0,1:T(8,128)} %copy-done.1, ...), kind=kLoop, calls=%fused_computation.25 | loop fusion | flops 20348928 | bytes 35782656 | tf_op jit(solution)/shard_map/mul | solution.py:56
  53.9 2.3 mul.78
  56.2 2.4 multiply_add_fusion
  58.9 11.4 %copy.10 = f32[12,8,8,4608]{3,2,0,1:T(8,128)} copy(f32[12,8,8,4608]{3,2,1,0:T(8,128)} %bitcast.31) | data formatting | bytes 28311552 | tf_op jit(solution)/shard_map/reshape | solution.py:58
  70.2 79.2 %all-gather.3.cloned.1.call-done = f32[32,55296]{1,0:T(8,128)} async-done(((f32[8,55296]{1,0:T(8,128)}), f32[32,55296]{1,0:T(8,128)}) %all-gather.3.cloned.1.call-update) | async-done | bytes 7077904 | tf_op jit(solution)/shard_map/all_gather | solution.py:59
  149.4 14.5 %convolution_bitcast_fusion = f32[64,32]{0,1:T(8,128)S(1)} fusion(f32[32,55296]{1,0:T(8,128)} %all-gather.3.cloned.1.call-done, f32[64,55296]{1,0:T(8,128)} %bitcast.27), kind=kOutput, calls=%fused_computation.63 | convolution fusion | flops 1358954496 | bytes 21241856 | tf_op jit(solution)/shard_map/dot_general | solution.py:43
  164.0 128.3 %psum.21 = f32[64,32]{0,1:T(8,128)S(1)} all-reduce(f32[64,32]{0,1:T(8,128)S(1)} %convolution_bitcast_fusion), channel_id=1, replica_groups=mesh['gx'=8,'gy'=4,'band'=4] {'gx','gy'}, use_global_device_ids=true, to_apply=%region_0.1 | all-reduce | flops 2048 | bytes 16384 | tf_op jit(solution)/shard_map/psum | solution.py:60
  292.3 11.7 %fusion.40 = f32[32,55296]{1,0:T(8,128)} fusion(f32[64,55296]{1,0:T(8,128)} %bitcast.28, f32[64,32]{0,1:T(8,128)S(1)} %psum.21), kind=kOutput, calls=%fused_computation.78 | convolution fusion | flops 1358956544 | bytes 21241856 | tf_op jit(solution)/shard_map/dot_general | solution.py:43
  304.0 66.2 %reduce-scatter.2.cloned.1.call-done = f32[8,55296]{1,0:T(8,128)} async-done(((f32[32,55296]{1,0:T(8,128)}), f32[8,55296]{1,0:T(8,128)}) %reduce-scatter.2.cloned.1.call-update) | async-done | bytes 1769488 | tf_op jit(solution)/shard_map/reduce_scatter | solution.py:61
  370.3 2.9 sub.3
  373.1 72.1 %all-gather.5.cloned.1.call-done = f32[32,55296]{1,0:T(8,128)} async-done(((f32[8,55296]{1,0:T(8,128)}), f32[32,55296]{1,0:T(8,128)}) %all-gather.5.cloned.1.call-update) | async-done | bytes 7077904 | tf_op jit(solution)/shard_map/all_gather | solution.py:65
  445.3 9.1 %fusion.49 = f32[32,32]{0,1:T(8,128)S(1)} fusion(f32[32,55296]{1,0:T(8,128)} %all-gather.5.cloned.1.call-done), kind=kOutput, calls=%fused_computation.91 | convolution fusion | flops 679477248 | bytes 7081984 | tf_op jit(solution)/shard_map/dot_general | solution.py:43
  454.4 25.5 %psum.22 = f32[32,32]{0,1:T(8,128)S(1)} all-reduce(f32[32,32]{0,1:T(8,128)S(1)} %fusion.49), channel_id=1, replica_groups=mesh['gx'=8,'gy'=4,'band'=4] {'gx'}, use_global_device_ids=true, to_apply=%region_2.3 | all-reduce | flops 1024 | bytes 8192 | tf_op jit(solution)/shard_map/psum | solution.py:66
  479.9 17.1 %psum.23 = f32[32,32]{0,1:T(8,128)S(1)} all-reduce(f32[32,32]{0,1:T(8,128)S(1)} %psum.22), channel_id=1, replica_groups=mesh['gx'=8,'gy'=4,'band'=4] {'gy'}, use_global_device_ids=true, to_apply=%region_3.4 | all-reduce | flops 1024 | bytes 8192 | tf_op jit(solution)/shard_map/psum | solution.py:66
  497.1 2.9 cholesky.17
  501.3 2.4 custom-call.6
  504.0 6.5 %fusion.43 = f32[8,55296]{1,0:T(8,128)} fusion(f32[32,55296]{1,0:T(8,128)} %all-gather.5.cloned.1.call-done, f32[32,32]{1,0:T(8,128)S(1)} %fusion.37, s32[]{:T(128)S(6)} %select_n.8), kind=kOutput, calls=%fused_computation.84 | convolution fusion | flops 169869312 | bytes 8851460 | tf_op jit(solution)/shard_map/dot_general | solution.py:43
  (33 shorter events, 6.6 us)
Async XLA Ops:
  6.5 142.9 %all-gather.3.cloned.1.call-start = ((), (), s32[]{:S(2)}) async-start(), calls=%async_computation.1 | async-start | bytes 8847360 | tf_op jit(solution)/shard_map/all_gather | solution.py:59
  8.5 3.5 copy-start.2
  8.7 3.2 collective-permute-start.1
  10.0 5.9 %collective-permute-start = (f32[8,4,24,192]{3,2,0,1:T(8,128)S(1)}, f32[8,4,24,192]{3,2,0,1:T(8,128)S(1)}, u32[]{:S(2)}, u32[]{:S(2)}) collective-permute-start(f32[8,4,24,192]{3,2,0,1:T(8,128)S(1)} %get-tuple-element.10), channel_id=1, source_target_pairs={{16,0},{32,16},{48,32},{64,48},{80,64},{96,80},{112,96},{17,1},{33... | collective-permute-start | bytes 1769480 | tf_op jit(solution)/shard_map/ppermute | solution.py:18
  12.9 3.5 copy-start.1
  16.1 17.1 %copy-start = (f32[8,16,24,192]{3,2,0,1:T(8,128)}, f32[8,16,24,192]{3,2,0,1:T(8,128)S(1)}, u32[]{:S(2)}) copy-start(f32[8,16,24,192]{3,2,0,1:T(8,128)S(1)} %get-tuple-element.12) | copy-start | bytes 7077892
  16.1 17.1 %copy-start.3 = (f32[8,20,24,192]{3,2,0,1:T(8,128)}, f32[8,20,24,192]{3,2,0,1:T(8,128)S(1)}, u32[]{:S(2)}) copy-start(f32[8,20,24,192]{3,2,0,1:T(8,128)S(1)} %get-tuple-element.13) | copy-start | bytes 8847364
  16.4 12.5 %collective-permute-start.2 = (f32[8,20,4,192]{3,2,0,1:T(4,128)S(1)}, f32[8,20,4,192]{3,2,0,1:T(4,128)S(1)}, u32[]{:S(2)}, u32[]{:S(2)}) collective-permute-start(f32[8,20,4,192]{3,2,0,1:T(4,128)S(1)} %get-tuple-element.5), channel_id=1, source_target_pairs={{4,0},{8,4},{12,8},{5,1},{9,5},{13,9},{6,2},{10,6},{14,10},{7,3},{... | collective-permute-start | bytes 1474568 | tf_op jit(solution)/shard_map/ppermute | solution.py:18
  17.7 12.6 %collective-permute-start.3 = (f32[8,20,4,192]{3,2,0,1:T(4,128)S(1)}, f32[8,20,4,192]{3,2,0,1:T(4,128)S(1)}, u32[]{:S(2)}, u32[]{:S(2)}) collective-permute-start(f32[8,20,4,192]{3,2,0,1:T(4,128)S(1)} %get-tuple-element.6), channel_id=1, source_target_pairs={{0,4},{4,8},{8,12},{1,5},{5,9},{9,13},{2,6},{6,10},{10,14},{3,7},{... | collective-permute-start | bytes 1474568 | tf_op jit(solution)/shard_map/ppermute | solution.py:17
  53.9 2.3 copy-start.5
  58.6 311.6 %reduce-scatter.2.cloned.1.call-start = ((), (), s32[]{:S(2)}) async-start(), calls=%async_computation.2 | async-start | bytes 8847360 | tf_op jit(solution)/shard_map/reduce_scatter | solution.py:61
  304.0 66.3 %copy-start.4 = (f32[8,12,4608]{2,0,1:T(8,128)S(1)}, f32[8,12,4608]{2,0,1:T(8,128)}, u32[]{:S(2)}) copy-start(f32[8,12,4608]{2,0,1:T(8,128)} %multiply_add_fusion) | copy-start | bytes 5308420
  304.0 141.3 %all-gather.5.cloned.1.call-start = ((), (), s32[]{:S(2)}) async-start(), calls=%async_computation.3 | async-start | bytes 8847360 | tf_op jit(solution)/shard_map/all_gather | solution.py:65
Sparse Core Ops, SparseCore 0:
  58.8 90.6 all-gather.2
  304.1 66.1 reduce-scatter.1
  373.3 71.9 all-gather.4
